TPU v7x, 32 devices: a whole 2x2x4 slice. The times are simulated.
32 devices in a mesh: mat: 4 (over z), pts: 8 (over y, x, core).
Axes of the slice: x: 2, y: 2, z: 4, core: 2. Of those that a mesh axis runs over, the one named last changes fastest.
Arguments:
- basis_values: bfloat16 [128, 2048, 512], P(('mat', 'pts')), may hold values from -6 to 6
- tile_ids: int32 [128, 4], P(('mat', 'pts')), may hold values from 0 to 3, as said below
- density_matrix: bfloat16 [512, 512], P('mat'), may hold values from -0.01171875 to 0.01171875
- descriptors: bfloat16 [128, 2048, 64], P(('mat', 'pts')), may hold values from -6 to 6
- grid_weights: float32 [128, 2048], P(('mat', 'pts')), may hold values from 0.25 to 2
- centre_ids: int32 [128, 2048], P(('mat', 'pts')), may hold values from 0 to 127
- density_scale: float32 [64], replicated, may hold values from -4 to 4
- norm_gain: float32 [64], replicated, may hold values from 0.1 to 1.9
- w_first: bfloat16 [64, 256], replicated, may hold values from -0.75 to 0.75
- b_first: float32 [256], replicated, may hold values from -3 to 3
- w_second: bfloat16 [256, 256], replicated, may hold values from -0.375 to 0.375
- b_second: float32 [256], replicated, may hold values from -3 to 3
- w_third: bfloat16 [256, 64], replicated, may hold values from -0.375 to 0.375
- b_third: float32 [64], replicated, may hold values from -3 to 3
Outputs:
- potential_matrix: bfloat16 [512, 512], P('mat', 'pts')
- centre_features: bfloat16 [128, 64], P('pts')
Inputs may be any that keep to these rules, and one draw needn't show every extreme that they name: `tile_ids`: the 4 tiles t of one batch have 4 different values of t.
All inputs are finite; a program needn't handle non-finite values.
Results may differ from a plain program's by a relative error of at most 0.0064.
Values may be sent and summed in bfloat16 or wider, within the bound.
A program may use at most 64 MiB of HBM per device.

v0:
```python
import math

import jax
import jax.numpy as jnp
from jax import lax
from jax.sharding import PartitionSpec as P

CENT_DEV = 16


def centre_network(summed, norm_gain, w_first, b_first, w_second, b_second, w_third, b_third):
    inverse = lax.rsqrt(jnp.mean(summed * summed, axis=1, keepdims=True) + 1e-05)
    normed = (summed * inverse * norm_gain).astype(jnp.bfloat16)
    hidden_one = jax.nn.silu(
        jnp.dot(normed, w_first, preferred_element_type=jnp.float32) + b_first
    ).astype(jnp.bfloat16)
    hidden_two = jax.nn.silu(
        jnp.dot(hidden_one, w_second, preferred_element_type=jnp.float32) + b_second
    ).astype(jnp.bfloat16)
    return (jnp.dot(hidden_two, w_third, preferred_element_type=jnp.float32) + b_third).astype(
        jnp.bfloat16
    )


def shards(
    basis_values,
    tile_ids,
    density_matrix,
    descriptors,
    grid_weights,
    centre_ids,
    density_scale,
    norm_gain,
    w_first,
    b_first,
    w_second,
    b_second,
    w_third,
    b_third,
):
    batch_count, point_count, orbitals = basis_values.shape
    per_batch = tile_ids.shape[1]
    tile_size = orbitals // per_batch
    rows_dev, basis_count = density_matrix.shape
    tile_count = basis_count // tile_size
    feat_width = descriptors.shape[2]
    groups = lax.axis_size("mat")
    blank = jnp.zeros((batch_count, per_batch, tile_size, orbitals), jnp.bfloat16)
    portion = lax.all_gather(density_matrix, "mat", axis=0, tiled=True)
    tiles_here = portion.shape[0] // tile_size
    tiled = portion.reshape(tiles_here, tile_size, tile_count, tile_size)
    inside = (tile_ids >= 0) & (tile_ids < tiles_here)
    clipped = jnp.clip(tile_ids, 0, tiles_here - 1)
    chosen = tiled[clipped[:, :, None], :, tile_ids[:, None, :]]
    chosen = chosen.transpose(0, 1, 3, 2, 4).reshape(batch_count, per_batch, tile_size, orbitals)
    panels = jnp.where(inside[:, :, None, None], chosen, blank)
    panel_full = panels.reshape(batch_count, orbitals, orbitals)
    projected = jnp.einsum(
        "bpa,bac->bpc", basis_values, panel_full, preferred_element_type=jnp.float32
    )
    density = jnp.sum(basis_values.astype(jnp.float32) * projected, axis=2)
    radial_terms = descriptors.astype(jnp.float32)
    features = jax.nn.silu(density[:, :, None] * density_scale + radial_terms)
    weighted_feat = grid_weights[:, :, None] * features
    centre_count = CENT_DEV * lax.axis_size("pts")
    partial_value = jax.ops.segment_sum(
        weighted_feat.reshape(-1, feat_width), centre_ids.reshape(-1), num_segments=centre_count
    )
    summed = lax.psum_scatter(partial_value, "pts", scatter_dimension=0, tiled=True)
    total_sum = lax.psum(summed, "mat")
    centre_features = centre_network(
        total_sum, norm_gain, w_first, b_first, w_second, b_second, w_third, b_third
    )
    everyone = lax.all_gather(centre_features, "pts", axis=0, tiled=True)
    nearest = everyone[centre_ids].astype(jnp.float32)
    batches_all = batch_count * groups * lax.axis_size("pts")
    factor = tile_count / (per_batch * math.sqrt(point_count * feat_width * batches_all))
    point_potential = grid_weights * density * jnp.sum(nearest * radial_terms, axis=2) * factor
    weighted = (point_potential[:, :, None] * basis_values.astype(jnp.float32)).astype(jnp.bfloat16)
    blocks_out = jnp.einsum(
        "bpa,bpc->bac", basis_values, weighted, preferred_element_type=jnp.float32
    )
    tile_blocks = blocks_out.reshape(
        batch_count, per_batch, tile_size, per_batch, tile_size
    ).transpose(0, 1, 3, 2, 4)
    whole = jnp.zeros((tile_count, tile_size, tile_count, tile_size), jnp.float32)
    whole = whole.at[tile_ids[:, :, None], :, tile_ids[:, None, :]].add(tile_blocks)
    row_part = lax.psum_scatter(
        whole.reshape(basis_count, basis_count), "mat", scatter_dimension=0, tiled=True
    )
    potential_matrix = lax.psum_scatter(row_part, "pts", scatter_dimension=1, tiled=True).astype(
        jnp.bfloat16
    )
    return (potential_matrix, centre_features)


def solution(mesh):
    return jax.shard_map(
        shards,
        mesh=mesh,
        in_specs=(
            P(("mat", "pts"), None, None),
            P(("mat", "pts"), None),
            P("mat", None),
            P(("mat", "pts"), None, None),
            P(("mat", "pts"), None),
            P(("mat", "pts"), None),
            P(),
            P(),
            P(),
            P(),
            P(),
            P(),
            P(),
            P(),
        ),
        out_specs=(P("mat", "pts"), P("pts", None)),
        check_vma=False,
    )
```

profile of v0, /device:TPU:4, one launch (start us, length us, event | category | flops | bytes accessed | tf_op | source)
XLA Modules:
  0.0 288.6 jit_solution(2118823780527542600)
XLA Ops:
  7.2 0.7 fusion.21
  7.9 0.7 compare_and_fusion
  8.8 16.1 %all_gather.6 = bf16[512,512]{1,0:T(8,128)(2,1)S(1)} all-gather(bf16[128,512]{1,0:T(8,128)(2,1)} %param.16), channel_id=1, replica_groups=mesh['mat'=4,'pts'=8] {'mat'}, dimensions={0}, use_global_device_ids=true | all-gather | bytes 655360 | tf_op jit(solution)/shard_map/all_gather | solution.py:49
  24.9 0.1 reshape.57
  25.2 1.0 gather_fusion
  26.1 2.6 copy.38
  28.7 2.7 reshape.58
  31.4 11.5 %copy.36 = bf16[4,2048,512]{1,2,0:T(8,128)(2,1)} copy(bf16[4,2048,512]{2,1,0:T(8,128)(2,1)} %param.14) | data formatting | bytes 16777216 | tf_op args[0]
  43.1 9.5 %fusion = f32[4,2048]{1,0:T(4,128)S(1)} fusion(bf16[4,2048,512]{1,2,0:T(8,128)(2,1)} %copy.36, bf16[4,2048,512]{2,1,0:T(8,128)(2,1)} %param.14, bf16[4,512,512]{1,2,0:T(8,128)(2,1)S(1)} %reshape.58, pred[4,512]{1,0:T(4,128)(4,1)S(1)} %bitcast.55), kind=kOutput, calls=%fused_computation.6 | convolution fusion | flops 4308590592 | bytes 18909184 | tf_op jit(solution)/shard_map/bpa,bac->bpc/dot_general | solution.py:58
  52.7 0.7 multiply_multiply_fusion
  53.5 2.7 copy.45
  56.2 44.9 %scatter_custom_fusion = f32[128,64]{1,0:T(8,128)} fusion(s32[8192]{0:T(1024)S(1)} %bitcast.54, f32[8192,64]{1,0:T(8,128)} %bitcast.47, f32[]{:T(128)} %constant.10.clone.1), kind=kCustom, calls=%fused_computation.26 | custom fusion | flops 524288 | bytes 33280 | tf_op jit(solution)/shard_map/scatter-add | solution.py:66
  101.3 35.2 %reduce-scatter.6.cloned.1.call-done = f32[16,64]{1,0:T(8,128)} async-done(((f32[128,64]{1,0:T(8,128)}), f32[16,64]{1,0:T(8,128)}) %reduce-scatter.6.cloned.1.call-update) | async-done | bytes 4112 | tf_op jit(solution)/shard_map/reduce_scatter | solution.py:69
  136.5 11.9 %psum.7 = f32[16,64]{1,0:T(8,128)S(1)} all-reduce(f32[16,64]{1,0:T(8,128)} %reduce-scatter.6.cloned.1.call-done), channel_id=1, replica_groups=mesh['mat'=4,'pts'=8] {'mat'}, use_global_device_ids=true, to_apply=%region_3.4 | all-reduce | flops 1024 | bytes 8192 | tf_op jit(solution)/shard_map/psum | solution.py:70
  148.4 0.1 multiply_reduce_fusion
  148.6 0.2 multiply_convert_fusion.1
  148.8 0.3 fusion.11
  149.1 8.3 %all_gather.7 = bf16[128,64]{1,0:T(8,128)(2,1)S(1)} all-gather(bf16[16,64]{1,0:T(8,128)(2,1)S(1)} %fusion.11), channel_id=1, replica_groups=mesh['mat'=4,'pts'=8] {'pts'}, dimensions={0}, use_global_device_ids=true | all-gather | bytes 18432 | tf_op jit(solution)/shard_map/all_gather | solution.py:74
  157.5 24.0 %gather_fusion.1 = bf16[8192,64]{1,0:T(8,128)(2,1)S(1)} fusion(bf16[128,64]{1,0:T(8,128)(2,1)S(1)} %all_gather.7, s32[8192]{0:T(1024)S(1)} %broadcast_clamp_fusion), kind=kCustom, calls=%fused_computation.1 | custom fusion | bytes 2129920 | tf_op jit(solution)/shard_map/gather | solution.py:75
  181.5 1.9 copy.41
  183.4 1.9 fusion.8
  185.3 12.2 %fusion.5 = f32[4,512,512]{1,2,0:T(8,128)} fusion(bf16[4,2048,512]{2,1,0:T(8,128)(2,1)} %param.14, bf16[4,2048,512]{1,2,0:T(8,128)(2,1)} %copy.36, f32[4,2048]{1,0:T(4,128)S(1)} %multiply_multiply_fusion.1), kind=kOutput, calls=%fused_computation.12 | convolution fusion | flops 4307550208 | bytes 21004288 | tf_op jit(solution)/shard_map/bpa,bpc->bac/dot_general | solution.py:80
  197.6 5.2 %reshape.60 = f32[4,4,128,4,128]{2,1,4,3,0:T(4,128)} reshape(f32[4,512,512]{1,2,0:T(8,128)} %fusion.5) | data formatting | bytes 8388608 | tf_op jit(solution)/shard_map/reshape | solution.py:83
  202.8 5.2 %copy.42 = f32[4,4,4,128,128]{4,3,2,1,0:T(8,128)} copy(f32[4,4,4,128,128]{3,1,4,2,0:T(4,128)} %bitcast.44) | data formatting | bytes 8388608 | tf_op jit(solution)/shard_map/transpose | solution.py:85
  208.1 9.8 %scatter_fusion = f32[4,128,4,128]{3,1,2,0:T(8,128)S(1)} fusion(f32[4,128,4,128]{3,1,2,0:T(8,128)S(1)} %broadcast_in_dim.26, s32[64]{0:T(128)S(1)} %reshape.84, f32[64,128,128]{2,1,0:T(8,128)} %bitcast.43), kind=kCustom, calls=%fused_computation.3 | custom fusion | flops 1048576 | bytes 12583424 | tf_op jit(solution)/shard_map/scatter-add | solution.py:87
  218.0 0.7 copy.43
  218.7 1.1 copy.55
  219.8 25.5 %reduce-scatter.8.cloned.1.call-done = f32[128,512]{1,0:T(8,128)} async-done(((f32[512,512]{1,0:T(8,128)}), f32[128,512]{1,0:T(8,128)}) %reduce-scatter.8.cloned.1.call-update) | async-done | bytes 262160 | tf_op jit(solution)/shard_map/reduce_scatter | solution.py:88
  245.3 1.8 copy.46
  247.1 33.4 %reduce-scatter.10.cloned.1.call-done = f32[64,128]{1,0:T(8,128)} async-done(((f32[512,128]{1,0:T(8,128)}), f32[64,128]{1,0:T(8,128)}) %reduce-scatter.10.cloned.1.call-update) | async-done | bytes 32784
  280.5 0.9 copy.47
  281.4 0.7 copy.44
  (43 shorter events, 0.8 us)
Async XLA Ops:
  7.2 141.6 %copy-start = (bf16[256,256]{1,0:T(8,128)(2,1)S(1)}, bf16[256,256]{1,0:T(8,128)(2,1)}, u32[]{:S(2)}) copy-start(bf16[256,256]{1,0:T(8,128)(2,1)} %param.24) | copy-start | bytes 393220
  7.2 129.3 %reduce-scatter.6.cloned.1.call-start = ((), (), s32[]{:S(2)}) async-start(), calls=%async_computation.3 | async-start | bytes 73728 | tf_op jit(solution)/shard_map/reduce_scatter | solution.py:69
  43.1 9.6 %copy-start.1 = (bf16[4,2048,64]{1,2,0:T(8,128)(2,1)S(1)}, bf16[4,2048,64]{1,2,0:T(8,128)(2,1)}, u32[]{:S(2)}) copy-start(bf16[4,2048,64]{1,2,0:T(8,128)(2,1)} %param.17) | copy-start | bytes 3145732
  43.1 9.6 %copy-start.2 = (f32[4,2048]{1,0:T(4,128)S(1)}, f32[4,2048]{1,0:T(4,128)}, u32[]{:S(2)}) copy-start(f32[4,2048]{1,0:T(4,128)} %param.18) | copy-start | bytes 98308
  43.1 9.6 %copy-start.8 = (f32[64]{0:T(128)S(1)}, f32[64]{0:T(128)}, u32[]{:S(2)}) copy-start(f32[64]{0:T(128)} %param.20) | copy-start | bytes 772
  53.4 2.8 copy-start.3
  53.4 95.2 %copy-start.9 = (bf16[64,256]{1,0:T(8,128)(2,1)S(1)}, bf16[64,256]{1,0:T(8,128)(2,1)}, u32[]{:S(2)}) copy-start(bf16[64,256]{1,0:T(8,128)(2,1)} %param.22) | copy-start | bytes 98308
  53.4 95.2 %copy-start.10 = (f32[256]{0:T(256)S(1)}, f32[256]{0:T(256)}, u32[]{:S(2)}) copy-start(f32[256]{0:T(256)} %param.23) | copy-start | bytes 3076
  53.4 95.2 %copy-start.11 = (f32[64]{0:T(128)S(1)}, f32[64]{0:T(128)}, u32[]{:S(2)}) copy-start(f32[64]{0:T(128)} %param.21) | copy-start | bytes 772
  53.4 95.4 %copy-start.4 = (bf16[256,64]{0,1:T(8,128)(2,1)S(1)}, bf16[256,64]{0,1:T(8,128)(2,1)}, u32[]{:S(2)}) copy-start(bf16[256,64]{0,1:T(8,128)(2,1)} %param.26) | copy-start | bytes 98308
  53.4 95.4 %copy-start.6 = (f32[256]{0:T(256)S(1)}, f32[256]{0:T(256)}, u32[]{:S(2)}) copy-start(f32[256]{0:T(256)} %param.25) | copy-start | bytes 3076
  53.4 95.4 %copy-start.7 = (f32[64]{0:T(128)S(1)}, f32[64]{0:T(128)}, u32[]{:S(2)}) copy-start(f32[64]{0:T(128)} %param.27) | copy-start | bytes 772
  101.1 144.2 %reduce-scatter.8.cloned.1.call-start = ((), (), s32[]{:S(2)}) async-start(), calls=%async_computation.4 | async-start | bytes 1310720 | tf_op jit(solution)/shard_map/reduce_scatter | solution.py:88
  149.1 32.4 %copy-start.5 = (bf16[16,64]{1,0:T(8,128)(2,1)}, bf16[16,64]{1,0:T(8,128)(2,1)S(1)}, u32[]{:S(2)}) copy-start(bf16[16,64]{1,0:T(8,128)(2,1)S(1)} %fusion.11) | copy-start | bytes 6148
  219.7 60.8 %reduce-scatter.10.cloned.1.call-start = ((), (), s32[]{:S(2)}) async-start(), calls=%async_computation.5 | async-start | bytes 294912
Sparse Core Ops, SparseCore 0:
  101.2 35.2 reduce-scatter.5
  219.9 25.3 reduce-scatter.7
  248.3 32.1 reduce-scatter.9
where the time goes:
time: 291 us; the launch traced here: 289 us
  waiting for transfers between devices  94.2 us (32%)
  local copies, waits for them, and re-layouts  62.7 us (22%)
  other arithmetic  59 us (20%)
  blocking collectives  36.4 us (13%)
  matrix products  22.3 us (8%)
  between operations  14.1 us (5%)
    scatter-add x1, other arithmetic, shards(): jax.ops.segment_sum(weighted_feat.reshape(-1, feat_width), centre_ids.res...  44.9 us
    reduce_scatter x1, waiting for transfers between devices, shards(): lax.psum_scatter(partial_value, 'pts', scatter_dimension=0, tiled=True)  35.2 us
    unnamed x4, waiting for transfers between devices  33.5 us
    reduce_scatter x1, waiting for transfers between devices, shards(): lax.psum_scatter(whole.reshape(basis_count, basis_count), 'mat', scatter_...  25.5 us
    gather x1, local copies, waits for them, and re-layouts, shards(): nearest = everyone[centre_ids].astype(jnp.float32)  24 us
    all_gather x1, blocking collectives, shards(): portion = lax.all_gather(density_matrix, 'mat', axis=0, tiled=True)  16.1 us
    unnamed x33, local copies, waits for them, and re-layouts  16.1 us
    dot_general x1, matrix products, shards(): jnp.einsum('bpa,bpc->bac', basis_values, weighted, preferred_element_type...  12.2 us
  transfers between devices with their start and end apart: 3, of which 3 were waited for; matrix products, arithmetic and copies ran while one was open for 0% of the time, Pallas kernels for 0%

commit v1 on v0

v1 whole, which is shorter than its diff:
```python
import functools
import math

import jax
import jax.numpy as jnp
from jax import lax
from jax.experimental import pallas as pl
from jax.experimental.pallas import tpu as pltpu
from jax.sharding import PartitionSpec as P

CHUNK = 512
SPLIT = 2
MESH = pl.DeviceIdType.MESH
F32 = jnp.float32
BF16 = jnp.bfloat16
NT_DIMS = (((1,), (1,)), ((), ()))


def silu(v):
    h = 0.5 * v
    return h + h * jnp.tanh(h)


def kernel(
    nm, npts, factor,
    v_hbm, d_hbm, tiles, dm, gw, ids, scale, gain, w1, b1, w2, b2, w3, b3,
    out_pot, out_cf,
    vbuf, dbuf, vt, dt, oh, gws, dens, pps, panel, cpart, cs_src, cs_in, cz_src, cz_in,
    full, cf_s, cft, acc, snd, rin, red, zsnd, zin,
    vsem, dsem, ag_s, ag_r, fw_s, fw_r, cs_s, cs_r, cz_s, cz_r, cg_s, cg_r, rp_s, rp_r, rz_s, rz_r,
):
    m = lax.axis_index("mat")
    p = lax.axis_index("pts")
    batches, points, orbitals = vbuf.shape
    per_batch = tiles.shape[1]
    tile = orbitals // per_batch
    rows, nb = dm.shape
    ntile = nb // tile
    feat = dbuf.shape[1]
    ncent = oh.shape[1]
    per = points // CHUNK
    chunks = batches * per
    slab = nb // npts
    piece = rows // SPLIT

    for b in range(batches):
        pltpu.make_async_copy(v_hbm.at[b], vbuf.at[b], vsem.at[b]).start()
        pltpu.make_async_copy(d_hbm.at[b], dbuf.at[b], dsem.at[b]).start()

    barrier = pltpu.get_barrier_semaphore()
    for k in range(1, npts):
        pl.semaphore_signal(barrier, inc=1, device_id={"pts": lax.rem(p + k, npts)}, device_id_type=MESH)
    for k in range(1, nm):
        pl.semaphore_signal(barrier, inc=1, device_id={"mat": lax.rem(m + k, nm)}, device_id_type=MESH)
    pl.semaphore_wait(barrier, npts + nm - 2)

    def remote(src, dst, s, r, **where):
        return pltpu.make_async_remote_copy(
            src_ref=src, dst_ref=dst, send_sem=s, recv_sem=r, device_id=where, device_id_type=MESH
        )

    def at_rows(owner, part):
        return pl.ds(pl.multiple_of(owner * rows + part * piece, piece), piece)

    g = lax.rem(p, SPLIT)
    base = p - g
    ag = []
    for k in range(1, nm):
        ag.append(remote(
            dm.at[pl.ds(pl.multiple_of(g * piece, piece), piece)], panel.at[at_rows(m, g)],
            ag_s.at[k - 1], ag_r.at[k - 1], mat=lax.rem(m + k, nm)))
    for c in ag:
        c.start()
    panel[pl.ds(pl.multiple_of(m * rows, rows), rows), :] = dm[...]

    def prepare(b):
        pltpu.make_async_copy(v_hbm.at[b], vbuf.at[b], vsem.at[b]).wait()
        pltpu.make_async_copy(d_hbm.at[b], dbuf.at[b], dsem.at[b]).wait()
        held = [tiles[b, j] for j in range(per_batch)]

        def body(i, carry):
            ch = b * per + i
            r0 = pl.multiple_of(i * CHUNK, CHUNK)
            for t in range(ntile):
                x = vbuf[b, pl.ds(r0, CHUNK), 0:tile]
                if ntile != per_batch:
                    x = jnp.where(held[0] == t, x, jnp.zeros_like(x))
                for j in range(1, per_batch):
                    x = jnp.where(held[j] == t, vbuf[b, pl.ds(r0, CHUNK), j * tile:(j + 1) * tile], x)
                x = x.T
                vt[ch, t * tile:(t + 1) * tile, :] = x
            dt[ch] = dbuf[b, :, pl.ds(r0, CHUNK)]
            row = ids[b:b + 1, pl.ds(r0, CHUNK)]
            which = lax.broadcasted_iota(jnp.int32, (ncent, CHUNK), 0)
            oh[ch] = jnp.where(which == row, 1.0, 0.0).astype(BF16)
            gws[ch] = gw[b:b + 1, pl.ds(r0, CHUNK)]
            return carry

        lax.fori_loop(0, per, body, 0)

    fw = []
    for b in range(batches):
        prepare(b)
        if b == min(1, batches - 1):
            for k in range(1, nm):
                ag[k - 1].wait_recv()
                held = panel.at[at_rows(lax.rem(m - k + nm, nm), g)]
                for s in range(1, SPLIT):
                    i = (k - 1) * (SPLIT - 1) + s - 1
                    c = remote(held, held, fw_s.at[i], fw_r.at[i], pts=base + lax.rem(g + s, SPLIT))
                    c.start()
                    fw.append(c)
    for c in fw:
        c.wait_recv()

    scale_col = jnp.broadcast_to(scale[...], (128, feat)).T[:, :1]
    cpart[...] = jnp.zeros_like(cpart)

    def density_step(ch, carry):
        x = vt[ch]
        q = jnp.dot(panel[...], x, preferred_element_type=F32)
        d = jnp.sum(q * x.astype(F32), axis=0, keepdims=True)
        dens[ch] = d
        wf = gws[ch] * silu(d * scale_col + dt[ch].astype(F32))
        high = wf.astype(BF16)
        low = (wf - high.astype(F32)).astype(BF16)
        both = lax.dot_general(
            jnp.concatenate([high, low], axis=0), oh[ch], NT_DIMS, preferred_element_type=F32)
        cpart[...] += both[:feat] + both[feat:]
        return carry

    lax.fori_loop(0, chunks, density_step, 0)

    fp = feat // npts
    for i in range(npts):
        cs_src[i] = cpart[i * fp:(i + 1) * fp, :]
    cs = []
    for k in range(1, npts):
        to = lax.rem(p + k, npts)
        c = remote(cs_src.at[to], cs_in.at[k - 1], cs_s.at[k - 1], cs_r.at[k - 1], pts=to)
        c.start()
        cs.append(c)
    mine = cs_src[p]
    for k in range(1, npts):
        cs[k - 1].wait_recv()
        mine = mine + cs_in[k - 1]
    cz_src[...] = mine
    cz = []
    for k in range(1, nm):
        c = remote(cz_src, cz_in.at[m], cz_s.at[k - 1], cz_r.at[k - 1], mat=lax.rem(m + k, nm))
        c.start()
        cz.append(c)
    cz_in[m] = mine
    for c in cz:
        c.wait_recv()
    total = cz_in[0]
    for i in range(1, nm):
        total = total + cz_in[i]
    full[p] = total
    cg = []
    for k in range(1, npts):
        c = remote(full.at[p], full.at[p], cg_s.at[k - 1], cg_r.at[k - 1], pts=lax.rem(p + k, npts))
        c.start()
        cg.append(c)
    for c in cg:
        c.wait_recv()

    summed = jnp.concatenate([full[i] for i in range(npts)], axis=0).T
    inverse = lax.rsqrt(jnp.mean(summed * summed, axis=1, keepdims=True) + 1e-05)
    normed = (summed * inverse * gain[...]).astype(BF16)
    one = silu(jnp.dot(normed, w1[...], preferred_element_type=F32) + b1[...]).astype(BF16)
    two = silu(jnp.dot(one, w2[...], preferred_element_type=F32) + b2[...]).astype(BF16)
    cf = (lax.dot_general(two, w3[...], NT_DIMS, preferred_element_type=F32) + b3[...]).astype(BF16).astype(F32)
    cf_s[...] = cf
    cft[...] = cf.T.astype(BF16)
    cent = out_cf.shape[0]
    out_cf[...] = cf_s[pl.ds(pl.multiple_of(p * cent, cent), cent), :].astype(BF16)

    half = nb // 2
    hp = npts // 2
    acc[...] = jnp.zeros_like(acc)
    rp = []
    for h in range(2):
        def block_step(ch, carry):
            if h == 0:
                near = jnp.dot(cft[...], oh[ch], preferred_element_type=F32)
                along = jnp.sum(near * dt[ch].astype(F32), axis=0, keepdims=True)
                pp = gws[ch] * dens[ch] * along * factor
                pps[ch] = pp
            else:
                pp = pps[ch]
            w = (vt[ch, h * half:(h + 1) * half, :].astype(F32) * pp).astype(BF16)
            r = lax.dot_general(w, vt[ch], NT_DIMS, preferred_element_type=F32)
            acc[h * hp:(h + 1) * hp] += r.reshape(hp, slab, nb)
            return carry

        lax.fori_loop(0, chunks, block_step, 0)
        for i in range(h * hp, (h + 1) * hp):
            snd[i] = acc[i].astype(BF16)
        for k in list(range(1, hp)) + [0]:
            to = h * hp + lax.rem(p + k, hp)
            c = remote(snd.at[to], rin.at[p], rp_s.at[to], rp_r.at[p], pts=to)
            rp.append((to, c))

            @pl.when(to != p)
            def _():
                c.start()

    mine = acc[p]
    for k in range(1, npts):
        src = lax.rem(p + k, npts)
        remote(snd.at[src], rin.at[src], rp_s.at[src], rp_r.at[src], pts=src).wait_recv()
        mine = mine + rin[src].astype(F32)
    width = nb // nm
    for j in range(nm):
        red[j] = mine[:, j * width:(j + 1) * width]
        zsnd[j] = mine[:, j * width:(j + 1) * width].astype(BF16)
    rz = []
    for k in range(1, nm):
        to = lax.rem(m + k, nm)
        c = remote(zsnd.at[to], zin.at[k - 1], rz_s.at[k - 1], rz_r.at[k - 1], mat=to)
        c.start()
        rz.append(c)
    mine = red[m]
    for k in range(1, nm):
        rz[k - 1].wait_recv()
        mine = mine + zin[k - 1].astype(F32)
    out_pot[...] = mine.astype(BF16)

    for c in ag + fw + cs + cz + cg + rz:
        c.wait_send()
    for to, c in rp:
        @pl.when(to != p)
        def _():
            c.wait_send()


def shards(
    nm, npts,
    basis_values, tile_ids, density_matrix, descriptors, grid_weights, centre_ids,
    density_scale, norm_gain, w_first, b_first, w_second, b_second, w_third, b_third,
):
    batches, points, orbitals = basis_values.shape
    per_batch = tile_ids.shape[1]
    tile = orbitals // per_batch
    rows, nb = density_matrix.shape
    feat = descriptors.shape[2]
    ntile = nb // tile
    cent = 16
    ncent = cent * npts
    chunks = batches * points // CHUNK
    slab = nb // npts
    width = nb // nm
    factor = ntile / (per_batch * math.sqrt(points * feat * batches * nm * npts))
    vm = pl.BlockSpec(memory_space=pltpu.VMEM)
    anyw = pl.BlockSpec(memory_space=pl.ANY)
    fp = feat // npts
    dma = pltpu.SemaphoreType.DMA
    nfw = (nm - 1) * (SPLIT - 1)
    potential, centre_features = pl.pallas_call(
        functools.partial(kernel, nm, npts, factor),
        out_shape=(
            jax.ShapeDtypeStruct((slab, width), BF16),
            jax.ShapeDtypeStruct((cent, feat), BF16),
        ),
        in_specs=[anyw, anyw, pl.BlockSpec(memory_space=pltpu.SMEM)] + [vm] * 11,
        out_specs=(vm, vm),
        scratch_shapes=[
            pltpu.VMEM((batches, points, orbitals), BF16),
            pltpu.VMEM((batches, feat, points), BF16),
            pltpu.VMEM((chunks, nb, CHUNK), BF16),
            pltpu.VMEM((chunks, feat, CHUNK), BF16),
            pltpu.VMEM((chunks, ncent, CHUNK), BF16),
            pltpu.VMEM((chunks, 1, CHUNK), F32),
            pltpu.VMEM((chunks, 1, CHUNK), F32),
            pltpu.VMEM((chunks, 1, CHUNK), F32),
            pltpu.VMEM((nb, nb), BF16),
            pltpu.VMEM((feat, ncent), F32),
            pltpu.VMEM((npts, fp, ncent), F32),
            pltpu.VMEM((npts, fp, ncent), F32),
            pltpu.VMEM((fp, ncent), F32),
            pltpu.VMEM((nm, fp, ncent), F32),
            pltpu.VMEM((npts, fp, ncent), F32),
            pltpu.VMEM((ncent, feat), F32),
            pltpu.VMEM((feat, ncent), BF16),
            pltpu.VMEM((npts, slab, nb), F32),
            pltpu.VMEM((npts, slab, nb), BF16),
            pltpu.VMEM((npts, slab, nb), BF16),
            pltpu.VMEM((nm, slab, width), F32),
            pltpu.VMEM((nm, slab, width), BF16),
            pltpu.VMEM((nm, slab, width), BF16),
            dma((batches,)), dma((batches,)),
            dma((nm - 1,)), dma((nm - 1,)),
            dma((nfw,)), dma((nfw,)),
            dma((npts - 1,)), dma((npts - 1,)),
            dma((nm - 1,)), dma((nm - 1,)),
            dma((npts - 1,)), dma((npts - 1,)),
            dma((npts,)), dma((npts,)),
            dma((nm - 1,)), dma((nm - 1,)),
        ],
        compiler_params=pltpu.CompilerParams(
            collective_id=0, has_side_effects=True, vmem_limit_bytes=60 * 1024 * 1024
        ),
    )(
        basis_values, descriptors.transpose(0, 2, 1), tile_ids, density_matrix, grid_weights, centre_ids,
        density_scale.reshape(1, -1), norm_gain.reshape(1, -1),
        w_first, b_first.reshape(1, -1), w_second, b_second.reshape(1, -1),
        w_third.T, b_third.reshape(1, -1),
    )
    return (potential.T, centre_features)


def solution(mesh):
    return jax.shard_map(
        functools.partial(shards, mesh.shape["mat"], mesh.shape["pts"]),
        mesh=mesh,
        in_specs=(
            P(("mat", "pts"), None, None),
            P(("mat", "pts"), None),
            P("mat", None),
            P(("mat", "pts"), None, None),
            P(("mat", "pts"), None),
            P(("mat", "pts"), None),
            P(), P(), P(), P(), P(), P(), P(), P(),
        ),
        out_specs=(P("mat", "pts"), P("pts", None)),
        check_vma=False,
    )
```

time: 291 us -> 63.4 us (0.22)
  waiting for transfers between devices: 94.2 us -> 0 us
  local copies, waits for them, and re-layouts: 62.7 us -> 2.59 us
  Pallas kernels: 0 us -> 59.9 us
  other arithmetic: 59 us -> 0 us
  blocking collectives: 36.4 us -> 0 us
  matrix products: 22.3 us -> 0 us
  between operations: 14.1 us -> 0.64 us
    reduce_scatter x2 -> x0, waiting for transfers between devices: 60.7 us -> none  [the longest x1 35.2 us: shards(): lax.psum_scatter(partial_value, 'pts', scatter_dimension=0, tiled=True)]
    pallas_call x0 -> x1, Pallas kernels: none -> 59.9 us  [shards(): pl.pallas_call(functools.partial(kernel, nm, npts, factor), out_shape=(ja...]
    scatter-add x2 -> x0, other arithmetic: 54.7 us -> none  [the longest x1 44.9 us: shards(): jax.ops.segment_sum(weighted_feat.reshape(-1, feat_width), centre_ids.res...]
    unnamed x4 -> x0, waiting for transfers between devices: 33.5 us -> none
    gather x2 -> x0, local copies, waits for them, and re-layouts: 25 us -> none  [the longest x1 24 us: shards(): nearest = everyone[centre_ids].astype(jnp.float32)]
    all_gather x2 -> x0, blocking collectives: 24.5 us -> none  [the longest x1 16.1 us: shards(): portion = lax.all_gather(density_matrix, 'mat', axis=0, tiled=True)]
    dot_general x4 -> x0, matrix products: 22.3 us -> none  [the longest x1 12.2 us: shards(): jnp.einsum('bpa,bpc->bac', basis_values, weighted, preferred_element_type...]
    unnamed x33 -> x2, local copies, waits for them, and re-layouts: 16.1 us -> 2.59 us
  transfers between devices with their start and end apart: 3 -> 0, of which waited for: 3 -> 0; matrix products, arithmetic and copies ran while one was open for 0% -> 0% of each run, Pallas kernels for 0% -> 0%
where the time goes in v1:
time: 63.4 us; the launch traced here: 63.1 us
  Pallas kernels  59.9 us (94%)
  local copies, waits for them, and re-layouts  2.59 us (4%)
  between operations  0.64 us (1%)
    pallas_call x1, Pallas kernels, shards(): pl.pallas_call(functools.partial(kernel, nm, npts, factor), out_shape=(ja...  59.9 us
    unnamed x2, local copies, waits for them, and re-layouts  2.59 us

profile of v1, /device:TPU:4, one launch (start us, length us, event | category | flops | bytes accessed | tf_op | source)
XLA Modules:
  0.0 63.1 jit_solution(13131873061005731827)
XLA Ops:
  0.6 59.9 %shard_map.149 = (bf16[64,128]{1,0:T(8,128)(2,1)}, bf16[16,64]{1,0:T(8,128)(2,1)}) custom-call(bf16[4,2048,512]{2,1,0:T(8,128)(2,1)} %v_hbm.1, bf16[4,64,2048]{2,1,0:T(8,128)(2,1)} %bitcast.8, s32[4,4]{1,0:T(4,128)} %tiles.1, bf16[128,512]{1,0:T(8,128)(2,1)} %dm.1, f32[4,2048]{1,0:T(4,128)} %gw.1, s32[4,2048]{1,0:T(4,128)} %ids.1, f32[1,64]{1,0:T(1,128)} %bitcast.13, ...), custom_call_target="tpu_custom_call" | custom-call | tf_op jit(solution)/shard_map/pallas_call | solution.py:260
  60.5 1.3 %copy.18 = bf16[128,64]{0,1:T(8,128)(2,1)} copy(bf16[128,64]{0,1:T(8,128)(2,1)} %bitcast.10) | data formatting | bytes 32768
  61.8 1.3 %copy.19 = bf16[16,64]{1,0:T(8,128)(2,1)} copy(bf16[16,64]{1,0:T(8,128)(2,1)} %get-tuple-element.9) | data formatting | bytes 4096

commit v2 on v1

--- a/solution.py
+++ b/solution.py
@@ -19,6 +19,11 @@
 def silu(v):
     h = 0.5 * v
     return h + h * jnp.tanh(h)
+
+
+def place(pot, cf, out_pot, out_cf):
+    out_pot[...] = pot[...]
+    out_cf[...] = cf[...]
 
 
 def kernel(
@@ -190,10 +195,14 @@
             else:
                 pp = pps[ch]
             w = (vt[ch, h * half:(h + 1) * half, :].astype(F32) * pp).astype(BF16)
-            r = lax.dot_general(w, vt[ch], NT_DIMS, preferred_element_type=F32)
-            acc[h * hp:(h + 1) * hp] += r.reshape(hp, slab, nb)
+            right = vt[ch] if h == 0 else vt[ch, half:, :]
+            r = lax.dot_general(w, right, NT_DIMS, preferred_element_type=F32)
+            acc[h * hp:(h + 1) * hp, :, h * half:] += r.reshape(hp, slab, nb - h * half)
             return carry
 
+        if h == 1:
+            corner = acc[:hp, :, half:].reshape(half, half)
+            acc[hp:, :, :half] = corner.T.reshape(hp, slab, half)
         lax.fori_loop(0, chunks, block_step, 0)
         for i in range(h * hp, (h + 1) * hp):
             snd[i] = acc[i].astype(BF16)
@@ -307,6 +316,15 @@
         w_first, b_first.reshape(1, -1), w_second, b_second.reshape(1, -1),
         w_third.T, b_third.reshape(1, -1),
     )
+    potential, centre_features = pl.pallas_call(
+        place,
+        out_shape=(
+            jax.ShapeDtypeStruct((slab, width), BF16),
+            jax.ShapeDtypeStruct((cent, feat), BF16),
+        ),
+        in_specs=[vm, vm],
+        out_specs=(vm, vm),
+    )(potential, centre_features)
     return (potential.T, centre_features)
 
 

time: 63.4 us -> 61 us (0.962)
  local copies, waits for them, and re-layouts: 2.59 us -> 0 us
    unnamed x2 -> x0, local copies, waits for them, and re-layouts: 2.59 us -> none
    pallas_call x0 -> x1, Pallas kernels: none -> 1.33 us  [shards(): pl.pallas_call(place, out_shape=(jax.ShapeDtypeStruct((slab, width), BF16...]
    pallas_call x1, Pallas kernels: 59.9 us -> 58.8 us  [shards(): pl.pallas_call(functools.partial(kernel, nm, npts, factor), out_shape=(ja...]
where the time goes in v2:
time: 61 us; the launch traced here: 60.8 us
  Pallas kernels  60.2 us (99%)
  between operations  0.64 us (1%)
    pallas_call x1, Pallas kernels, shards(): pl.pallas_call(functools.partial(kernel, nm, npts, factor), out_shape=(ja...  58.8 us
    pallas_call x1, Pallas kernels, shards(): pl.pallas_call(place, out_shape=(jax.ShapeDtypeStruct((slab, width), BF16...  1.33 us

profile of v2, /device:TPU:4, one launch (start us, length us, event | category | flops | bytes accessed | tf_op | source)
XLA Modules:
  0.0 60.8 jit_solution(12849876950956913234)
XLA Ops:
  0.6 58.8 %shard_map.149 = (bf16[64,128]{1,0:T(8,128)(2,1)}, bf16[16,64]{1,0:T(8,128)(2,1)}) custom-call(bf16[4,2048,512]{2,1,0:T(8,128)(2,1)} %v_hbm.1, bf16[4,64,2048]{2,1,0:T(8,128)(2,1)} %bitcast.8, s32[4,4]{1,0:T(4,128)} %tiles.1, bf16[128,512]{1,0:T(8,128)(2,1)} %dm.1, f32[4,2048]{1,0:T(4,128)} %gw.1, s32[4,2048]{1,0:T(4,128)} %ids.1, f32[1,64]{1,0:T(1,128)} %bitcast.12, ...), custom_call_target="tpu_custom_call" | custom-call | tf_op jit(solution)/shard_map/pallas_call | solution.py:269
  59.5 1.3 %shard_map.150 = (bf16[64,128]{1,0:T(8,128)(2,1)}, bf16[16,64]{1,0:T(8,128)(2,1)}) custom-call(bf16[64,128]{1,0:T(8,128)(2,1)} %get-tuple-element.6.pot, bf16[16,64]{1,0:T(8,128)(2,1)} %get-tuple-element.7.cf), custom_call_target="tpu_custom_call" | custom-call | tf_op jit(solution)/shard_map/pallas_call | solution.py:319
